TPU v7x, 32 devices: a whole 2x2x4 slice. The times are simulated.
32 devices in a mesh: section: 4 (over z), ctx: 8 (over y, x, core).
Axes of the slice: x: 2, y: 2, z: 4, core: 2. Of those that a mesh axis runs over, the one named last changes fastest.
Arguments:
- stream: bfloat16 [1024, 2688], P('ctx'), may hold values from -6 to 6
- queries: bfloat16 [4, 1024, 2048], P('section', 'ctx'), may hold values from -51 to 51
- keys: bfloat16 [4, 1024, 1024], P('section', 'ctx'), may hold values from -4 to 4
- values: bfloat16 [4, 1024, 1024], P('section', 'ctx'), may hold values from -120 to 120
- out_weight: bfloat16 [4, 2048, 2688], P('section', 'ctx'), may hold values from -0.125 to 0.125
- gains: bfloat16 [4, 2688], P('section'), may hold values from 0.099609375 to 1.8984375
Outputs:
- layer_outputs: bfloat16 [4, 1024, 2688], P('section', 'ctx')
All inputs are finite; a program needn't handle non-finite values.
Results may differ from a plain program's by a relative error of at most 0.009.
Values may be sent and summed in bfloat16 or wider, within the bound.
A program may use at most 64 MiB of HBM per device.

v0:
```python
import functools
import math

import jax
import jax.numpy as jnp
from jax import lax
from jax.experimental import pallas as pl
from jax.experimental.pallas import tpu as pltpu
from jax.sharding import PartitionSpec as P

KEY_HEADS = 8
HEAD_WIDTH = 128
WINDOW_LENGTH = 1024
QUERY_SCALAR = 168
QUERY_PER_KEY = 2


norm_eps = 1e-06


def passed_along(block, axis, distance):
    devices = range(lax.axis_size(axis))
    route = [(i - distance, i) for i in devices if i - distance in devices]
    return lax.ppermute(block, axis, route)


def attend_block(query_matrix_rows, key_matrix_rows, value_matrix_rows, allowed, scale_factor):
    scores = (
        jnp.einsum(
            "qhgd,khd->hgqk", query_matrix_rows, key_matrix_rows, preferred_element_type=jnp.float32
        )
        * scale_factor
    )
    scores = jnp.where(allowed, scores, -jnp.inf)
    row_top = jnp.max(scores, axis=-1, keepdims=True)
    exponent = jnp.exp(scores - row_top)
    row_total = jnp.sum(exponent, axis=-1, keepdims=True)
    weights = exponent.astype(jnp.bfloat16)
    mixed_rows = jnp.einsum(
        "hgqk,khd->qhgd", weights, value_matrix_rows, preferred_element_type=jnp.float32
    )
    return mixed_rows / jnp.transpose(row_total, (2, 0, 1, 3))


def local(stream, queries, keys, values, out_weight, gains):
    tok_rows = stream.shape[0]
    span_rows = min(tok_rows, WINDOW_LENGTH)
    hop_count = WINDOW_LENGTH // span_rows
    own_tail = (keys[0, tok_rows - span_rows :], values[0, tok_rows - span_rows :])
    pieces = [
        passed_along((own_tail[0], own_tail[1]), "ctx", distance)
        for distance in range(hop_count, 0, -1)
    ]
    key_matrix_rows = jnp.concatenate([piece_pair[0] for piece_pair in pieces] + [keys[0]], axis=0)
    value_matrix_rows = jnp.concatenate(
        [piece_pair[1] for piece_pair in pieces] + [values[0]], axis=0
    )
    ctx_base = lax.axis_index("ctx") * tok_rows
    query_pos = ctx_base + jnp.arange(tok_rows, dtype=jnp.int32)
    key_pos = ctx_base - WINDOW_LENGTH + jnp.arange(WINDOW_LENGTH + tok_rows, dtype=jnp.int32)
    allowed = (
        (key_pos[None, :] >= 0)
        & (key_pos[None, :] <= query_pos[:, None])
        & (key_pos[None, :] > query_pos[:, None] - WINDOW_LENGTH)
    )
    scale_factor = QUERY_SCALAR ** (-0.5)
    heads_per_block = math.gcd(KEY_HEADS, 4)
    query_width = heads_per_block * QUERY_PER_KEY * HEAD_WIDTH
    key_width = heads_per_block * HEAD_WIDTH
    outputs_list = []
    for query_head_group in range(KEY_HEADS // heads_per_block):
        query_cols = queries[
            0, :, query_head_group * query_width : (query_head_group + 1) * query_width
        ].reshape(tok_rows, heads_per_block, QUERY_PER_KEY, HEAD_WIDTH)
        key_cols = key_matrix_rows[
            :, query_head_group * key_width : (query_head_group + 1) * key_width
        ].reshape(WINDOW_LENGTH + tok_rows, heads_per_block, HEAD_WIDTH)
        value_cols = value_matrix_rows[
            :, query_head_group * key_width : (query_head_group + 1) * key_width
        ].reshape(WINDOW_LENGTH + tok_rows, heads_per_block, HEAD_WIDTH)
        mixed_rows = attend_block(query_cols, key_cols, value_cols, allowed, scale_factor)
        outputs_list.append(mixed_rows.reshape(tok_rows, query_width))
    attended = jnp.concatenate(outputs_list, axis=1).astype(jnp.bfloat16)
    projected = jnp.dot(
        attended,
        lax.all_gather(out_weight[0], "ctx", axis=0, tiled=True),
        preferred_element_type=jnp.float32,
    )
    mean_square = jnp.mean(projected * projected, axis=-1, keepdims=True)
    branch = projected * lax.rsqrt(mean_square + norm_eps) * gains[0].astype(jnp.float32)
    section_index = lax.axis_index("section")
    section_count = lax.axis_size("section")
    running = jnp.where(
        section_index == 0, stream.astype(jnp.float32) + branch, jnp.zeros_like(branch)
    )
    for turn_index in range(section_count - 1):
        arrived = passed_along(running.astype(jnp.bfloat16), "section", 1).astype(running.dtype)
        running = jnp.where(section_index == turn_index + 1, arrived + branch, running)
    return running.astype(jnp.bfloat16)[None]


LANES = 128
MESH = pl.DeviceIdType.MESH
CHUNKS = 8
PARTS = 2
LEAD = 2
VMEM_GRANT = 66_300_000


def column_tiles(start, stop, width):
    return [(at, min(at + width, stop) - at) for at in range(start, stop, width)]


def fused_kernel(
    sections,
    chunks,
    parts,
    half,
    gains_hbm,
    stream_ref,
    q_ref,
    k_ref,
    v_ref,
    w_hbm,
    out_ref,
    qbuf,
    kbuf,
    vbuf,
    w_ref,
    gains_ref,
    att,
    pair_out,
    pair_in,
    x1_out,
    x1_in,
    y1_out,
    y1_in,
    x2_out,
    x2_in,
    y2_out,
    y2_in,
    keep_me,
    keep_x,
    keep_y,
    base,
    local_sem,
    a2a_send,
    a2a_recv,
    pair_sem,
    x1_sem,
    y1_sem,
    x2_sem,
    y2_sem,
    chain_sem,
):
    me = lax.axis_index("ctx")
    section = lax.axis_index("section")
    devices, rows, query_width = qbuf.shape
    width = w_ref.shape[1]
    chunk_rows = rows // chunks
    quarter, pair_count = devices // 4, devices // 2
    core = me % 2
    across = (me // quarter) % 2
    up = me // pair_count
    flips = (1 - 2 * core, quarter * (1 - 2 * across), pair_count * (1 - 2 * up))

    def peer(flip_core, flip_x, flip_y):
        return me + flips[0] * flip_core + flips[1] * flip_x + flips[2] * flip_y

    sibling, beside, above, diagonal = peer(1, 0, 0), peer(0, 1, 0), peer(0, 0, 1), peer(0, 1, 1)
    has_prev = jnp.minimum(section, 1)
    has_next = jnp.minimum(sections - 1 - section, 1)

    def own_rows(buf):
        return buf.at[pl.ds(pl.multiple_of(me * rows, rows), rows)]

    def head_columns(ref, who, span):
        return ref.at[:, pl.ds(pl.multiple_of(who * span, span), span)]

    w_copy = pltpu.make_async_copy(w_hbm, w_ref, local_sem.at[0])
    w_copy.start()
    gains_copy = pltpu.make_async_copy(gains_hbm, gains_ref, local_sem.at[1])
    gains_copy.start()

    @pl.when(section == 0)
    def _():
        for chunk in range(chunks):
            pltpu.make_async_copy(
                stream_ref.at[pl.ds(chunk * chunk_rows, chunk_rows)],
                base.at[chunk],
                chain_sem.at[1, chunk],
            ).start()

    part_rows = rows // parts

    def query_part(who, part):
        source = q_ref.at[
            pl.ds(part * part_rows, part_rows),
            pl.ds(pl.multiple_of(who * query_width, query_width), query_width),
        ]
        return source, qbuf.at[me, pl.ds(part * part_rows, part_rows)]

    def pieces(who):
        return [
            (head_columns(k_ref, who, HEAD_WIDTH), own_rows(kbuf)),
            (head_columns(v_ref, who, HEAD_WIDTH), own_rows(vbuf)),
        ] + [query_part(who, part) for part in range(parts)]

    for which, (source, target) in enumerate(pieces(me)):
        pltpu.make_async_copy(source, target, a2a_recv.at[which, me]).start()

    order = [(0, 1, 1), (1, 1, 1), (0, 1, 0), (0, 0, 1), (1, 1, 0), (1, 0, 1), (1, 0, 0)]
    barrier = pltpu.get_barrier_semaphore()
    for flip in order:
        pl.semaphore_signal(barrier, inc=1, device_id=(section, peer(*flip)), device_id_type=MESH)

    @pl.when(section > 0)
    def _():
        pl.semaphore_signal(barrier, inc=1, device_id=(section - 1, me), device_id_type=MESH)

    @pl.when(section < sections - 1)
    def _():
        pl.semaphore_signal(barrier, inc=1, device_id=(section + 1, me), device_id_type=MESH)

    pl.semaphore_wait(barrier, len(order) + has_prev + has_next)

    def exchange(who):
        return [
            pltpu.make_async_remote_copy(
                src_ref=source,
                dst_ref=target,
                send_sem=a2a_send.at[which, who],
                recv_sem=a2a_recv.at[which, me],
                device_id=(section, who),
                device_id_type=MESH,
            )
            for which, (source, target) in enumerate(pieces(who))
        ]

    exchanges = [exchange(peer(*flip)) for flip in order]
    for wave in zip(*exchanges):
        for copy in wave:
            copy.start()

    def arrive(which, target, block):
        pltpu.make_async_copy(target, target, a2a_recv.at[which, block]).wait()

    factor = QUERY_SCALAR ** (-0.5) * math.log2(math.e)
    group = query_width // HEAD_WIDTH
    part_chunks = chunks // parts

    def attend(part):
        low = pl.multiple_of(part * part_rows, part_rows)
        place = lax.broadcasted_iota(jnp.int32, (group, part_rows, rows), 1) + low
        seen = lax.broadcasted_iota(jnp.int32, (group, part_rows, rows), 2) <= place
        seen = seen.reshape(group * part_rows, rows)
        for block in range(devices):

            @pl.when(part == 0)
            def _():
                arrive(0, kbuf.at[pl.ds(block * rows, rows)], block)
                arrive(1, vbuf.at[pl.ds(block * rows, rows)], block)

            arrive(2 + part, qbuf.at[block, pl.ds(low, part_rows)], block)

        for block in range(devices):
            reach = (block + 1) * rows
            asked = jnp.concatenate(
                [
                    qbuf[block, pl.ds(low, part_rows), head * HEAD_WIDTH : (head + 1) * HEAD_WIDTH]
                    for head in range(group)
                ],
                axis=0,
            )
            scores = lax.dot_general(
                asked,
                kbuf[0:reach],
                (((1,), (1,)), ((), ())),
                preferred_element_type=jnp.float32,
            )
            last = jnp.where(seen, scores[:, block * rows :], -jnp.inf)
            if block:
                scores = jnp.concatenate([scores[:, : block * rows], last], axis=1)
            else:
                scores = last
            top = jnp.max(scores, axis=1, keepdims=True)
            exponent = jnp.exp2((scores - top) * factor)
            total = jnp.sum(exponent, axis=1, keepdims=True)
            mixed = jnp.dot(
                exponent.astype(jnp.bfloat16), vbuf[0:reach], preferred_element_type=jnp.float32
            )
            mixed = (mixed / total).astype(jnp.bfloat16)
            for head in range(group):
                for chunk in range(part_chunks):
                    start = head * part_rows + chunk * chunk_rows
                    att[
                        block % 2,
                        part * part_chunks + chunk,
                        block // 2,
                        :,
                        head * HEAD_WIDTH : (head + 1) * HEAD_WIDTH,
                    ] = mixed[start : start + chunk_rows]

    def remote(source, target, sems, chunk, who):
        return pltpu.make_async_remote_copy(
            src_ref=source.at[chunk],
            dst_ref=target.at[chunk],
            send_sem=sems.at[0, chunk],
            recv_sem=sems.at[1, chunk],
            device_id=who,
            device_id_type=MESH,
        )

    def pair_copy(chunk):
        return remote(pair_out, pair_in, pair_sem, chunk, (section, sibling))

    def x1_copy(chunk):
        return remote(x1_out, x1_in, x1_sem, chunk, (section, beside))

    def y1_copy(chunk):
        return remote(y1_out, y1_in, y1_sem, chunk, (section, above))

    def x2_copy(chunk):
        return remote(x2_out, x2_in, x2_sem, chunk, (section, beside))

    def y2_copy(chunk):
        return remote(y2_out, y2_in, y2_sem, chunk, (section, above))

    def chain_copy(chunk):
        return pltpu.make_async_remote_copy(
            src_ref=out_ref.at[chunk],
            dst_ref=base.at[chunk],
            send_sem=chain_sem.at[0, chunk],
            recv_sem=chain_sem.at[1, chunk],
            device_id=(jnp.minimum(section + 1, sections - 1), me),
            device_id_type=MESH,
        )

    chip_count = pair_count
    places = [who // 2 for who in (beside, diagonal, above, me)]

    def for_sibling(chunk):
        left = att[1 - core, chunk].reshape(chip_count * chunk_rows, query_width)
        for at, span in column_tiles(0, width, 512):
            part = jnp.dot(left, w_ref[:, at : at + span], preferred_element_type=jnp.float32)
            pair_out[chunk, :, :, at : at + span] = part.astype(jnp.bfloat16).reshape(
                chip_count, chunk_rows, span
            )
        pair_copy(chunk).start()

    def first_turn(chunk):
        pair_copy(chunk).wait_recv()
        left = jnp.concatenate([att[core, chunk, place] for place in places], axis=0)

        def summed(at, span):
            part = jnp.dot(left, w_ref[:, at : at + span], preferred_element_type=jnp.float32)
            return [
                part[index * chunk_rows : (index + 1) * chunk_rows]
                + pair_in[chunk, place, :, at : at + span].astype(jnp.float32)
                for index, place in enumerate(places)
            ]

        for at, span in column_tiles(0, half, 512):
            to_beside, to_diagonal, to_above, mine = summed(at, span)
            x1_out[chunk, 0, :, at : at + span] = to_beside.astype(jnp.bfloat16)
            x1_out[chunk, 1, :, at : at + span] = to_diagonal.astype(jnp.bfloat16)
            keep_y[chunk, :, at : at + span] = to_above
            keep_me[chunk, :, at : at + span] = mine
        x1_copy(chunk).start()
        for at, span in column_tiles(half, width, 512):
            to_beside, to_diagonal, to_above, mine = summed(at, span)
            y1_out[chunk, 0, :, at - half : at - half + span] = to_above.astype(jnp.bfloat16)
            y1_out[chunk, 1, :, at - half : at - half + span] = to_diagonal.astype(jnp.bfloat16)
            keep_x[chunk, :, at - half : at - half + span] = to_beside
            keep_me[chunk, :, at : at + span] = mine
        y1_copy(chunk).start()

    def second_turn(chunk):
        x1_copy(chunk).wait_recv()
        y2_out[chunk] = (keep_y[chunk] + x1_in[chunk, 1].astype(jnp.float32)).astype(jnp.bfloat16)
        y2_copy(chunk).start()
        y1_copy(chunk).wait_recv()
        x2_out[chunk] = (keep_x[chunk] + y1_in[chunk, 1].astype(jnp.float32)).astype(jnp.bfloat16)
        x2_copy(chunk).start()
        keep_me[chunk, :, :half] += x1_in[chunk, 0].astype(jnp.float32)
        keep_me[chunk, :, half:] += y1_in[chunk, 0].astype(jnp.float32)

    def normalise(chunk):
        y2_copy(chunk).wait_recv()
        x2_copy(chunk).wait_recv()
        low = keep_me[chunk, :, :half] + y2_in[chunk].astype(jnp.float32)
        high = keep_me[chunk, :, half:] + x2_in[chunk].astype(jnp.float32)
        squares = jnp.sum(low * low, axis=1, keepdims=True) + jnp.sum(
            high * high, axis=1, keepdims=True
        )
        ratio = lax.rsqrt(squares * (1.0 / width) + norm_eps)
        keep_me[chunk, :, :half] = low * ratio * gains_ref[:, :half].astype(jnp.float32)
        keep_me[chunk, :, half:] = high * ratio * gains_ref[:, half:].astype(jnp.float32)

    def hand_on(chunk):
        pltpu.make_async_copy(base.at[chunk], base.at[chunk], chain_sem.at[1, chunk]).wait()
        out_ref[chunk] = (base[chunk].astype(jnp.float32) + keep_me[chunk]).astype(out_ref.dtype)

        @pl.when(section < sections - 1)
        def _():
            chain_copy(chunk).start()

    def turn(ahead, carry):
        step = ahead - LEAD

        @pl.when((ahead % part_chunks == 0) & (ahead < chunks))
        def _():
            attend(ahead // part_chunks)

        @pl.when(step == 0)
        def _():
            w_copy.wait()
            gains_copy.wait()

        for lag, stage in enumerate((for_sibling, first_turn, second_turn, normalise)):
            chunk = step - lag

            @pl.when((chunk >= 0) & (chunk < chunks))
            def _():
                stage(chunk)

        passed = step - 3 - section

        @pl.when((passed >= 0) & (passed < chunks))
        def _():
            hand_on(passed)

        return carry

    lax.fori_loop(0, LEAD + chunks + 3 + sections - 1, turn, 0)

    for wave in exchanges:
        for copy in wave:
            copy.wait_send()

    def finish(chunk, carry):
        for copy in (pair_copy, x1_copy, y1_copy, x2_copy, y2_copy):
            copy(chunk).wait_send()

        @pl.when(section < sections - 1)
        def _():
            chain_copy(chunk).wait_send()

        return carry

    lax.fori_loop(0, chunks, finish, 0)


def by_head(sections, chunks, parts, stream, queries, keys, values, out_weight, gains):
    devices = lax.axis_size("ctx")
    rows, width = stream.shape
    query_width = queries.shape[2] // devices
    chunk_rows = rows // chunks
    half = (width // LANES + 1) // 2 * LANES
    other = width - half
    chips = devices // 2
    narrow, wide = jnp.bfloat16, jnp.float32
    anywhere = pl.BlockSpec(memory_space=pl.ANY)
    in_vmem = pl.BlockSpec(memory_space=pltpu.VMEM)
    dma = pltpu.SemaphoreType.DMA
    out = pl.pallas_call(
        functools.partial(fused_kernel, sections, chunks, parts, half),
        out_shape=jax.ShapeDtypeStruct((chunks, chunk_rows, width), narrow),
        in_specs=[anywhere] * 6,
        out_specs=in_vmem,
        scratch_shapes=[
            pltpu.VMEM((devices, rows, query_width), narrow),
            pltpu.VMEM((devices * rows, HEAD_WIDTH), narrow),
            pltpu.VMEM((devices * rows, HEAD_WIDTH), narrow),
            pltpu.VMEM(out_weight.shape[1:], narrow),
            pltpu.VMEM(gains.shape, narrow),
            pltpu.VMEM((2, chunks, chips, chunk_rows, query_width), narrow),
            pltpu.VMEM((chunks, chips, chunk_rows, width), narrow),
            pltpu.VMEM((chunks, chips, chunk_rows, width), narrow),
            pltpu.VMEM((chunks, 2, chunk_rows, half), narrow),
            pltpu.VMEM((chunks, 2, chunk_rows, half), narrow),
            pltpu.VMEM((chunks, 2, chunk_rows, other), narrow),
            pltpu.VMEM((chunks, 2, chunk_rows, other), narrow),
            pltpu.VMEM((chunks, chunk_rows, other), narrow),
            pltpu.VMEM((chunks, chunk_rows, other), narrow),
            pltpu.VMEM((chunks, chunk_rows, half), narrow),
            pltpu.VMEM((chunks, chunk_rows, half), narrow),
            pltpu.VMEM((chunks, chunk_rows, width), wide),
            pltpu.VMEM((chunks, chunk_rows, other), wide),
            pltpu.VMEM((chunks, chunk_rows, half), wide),
            pltpu.VMEM((chunks, chunk_rows, width), narrow),
            dma((2,)),
            dma((2 + parts, devices)),
            dma((2 + parts, devices)),
            dma((2, chunks)),
            dma((2, chunks)),
            dma((2, chunks)),
            dma((2, chunks)),
            dma((2, chunks)),
            dma((2, chunks)),
        ],
        compiler_params=pltpu.CompilerParams(
            collective_id=0, has_side_effects=True, vmem_limit_bytes=VMEM_GRANT
        ),
    )(gains, stream, queries[0], keys[0], values[0], out_weight[0])
    return out.reshape(1, rows, width)


def fits_by_head(mesh, rows):
    devices = mesh.shape["ctx"]
    return devices == KEY_HEADS and devices * rows <= WINDOW_LENGTH and devices % 8 == 0


def solution(mesh):
    in_specs = (
        P("ctx", None),
        P("section", "ctx", None),
        P("section", "ctx", None),
        P("section", "ctx", None),
        P("section", "ctx", None),
        P("section", None),
    )
    out_specs = P("section", "ctx", None)
    sections = mesh.shape["section"]

    def step(stream, *rest):
        rows = stream.shape[0]
        if fits_by_head(mesh, rows):
            return by_head(sections, CHUNKS, PARTS, stream, *rest)
        return local(stream, *rest)

    return jax.shard_map(step, mesh=mesh, in_specs=in_specs, out_specs=out_specs, check_vma=False)
```

profile of v0, /device:TPU:24, one launch (start us, length us, event | category | flops | bytes accessed | tf_op | source)
XLA Modules:
  0.0 59.4 jit_solution(13408432500381966974)
XLA Ops:
  0.0 57.3 %shard_map.64 = bf16[8,16,2688]{2,1,0:T(8,128)(2,1)} custom-call(bf16[1,2688]{1,0:T(2,128)(2,1)} %gains_hbm.1, bf16[128,2688]{1,0:T(8,128)(2,1)} %stream_ref.1, bf16[128,2048]{1,0:T(8,128)(2,1)} %bitcast.7, bf16[128,1024]{1,0:T(8,128)(2,1)} %bitcast.8, bf16[128,1024]{1,0:T(8,128)(2,1)} %bitcast.9, bf16[256,2688]{1,0:T(8,128)(2,1)} %bitcast.6), custom_call_target="tpu_custom_call" | custom-call | tf_op jit(solution)/shard_map/pallas_call | solution.py:466
  57.4 2.0 %copy.8 = bf16[1,128,2688]{2,1,0:T(8,128)(2,1)} copy(bf16[1,128,2688]{2,1,0:T(8,128)(2,1)} %bitcast.5) | data formatting | bytes 1376256
where the time goes:
time: 59.5 us; the launch traced here: 59.4 us
  Pallas kernels  57.3 us (96%)
  local copies, waits for them, and re-layouts  1.99 us (3%)
    pallas_call x1, Pallas kernels, by_head(): pl.pallas_call(functools.partial(fused_kernel, sections, chunks, parts, h...  57.3 us
    unnamed x1, local copies, waits for them, and re-layouts  1.99 us

commit v1 on v0

v1 whole, which is shorter than its diff:
```python
import functools
import math

import jax
import jax.numpy as jnp
from jax import lax
from jax.experimental import pallas as pl
from jax.experimental.pallas import tpu as pltpu
from jax.sharding import PartitionSpec as P

KEY_HEADS = 8
HEAD_WIDTH = 128
WINDOW_LENGTH = 1024
QUERY_SCALAR = 168
QUERY_PER_KEY = 2


norm_eps = 1e-06


def passed_along(block, axis, distance):
    devices = range(lax.axis_size(axis))
    route = [(i - distance, i) for i in devices if i - distance in devices]
    return lax.ppermute(block, axis, route)


def attend_block(query_matrix_rows, key_matrix_rows, value_matrix_rows, allowed, scale_factor):
    scores = (
        jnp.einsum(
            "qhgd,khd->hgqk", query_matrix_rows, key_matrix_rows, preferred_element_type=jnp.float32
        )
        * scale_factor
    )
    scores = jnp.where(allowed, scores, -jnp.inf)
    row_top = jnp.max(scores, axis=-1, keepdims=True)
    exponent = jnp.exp(scores - row_top)
    row_total = jnp.sum(exponent, axis=-1, keepdims=True)
    weights = exponent.astype(jnp.bfloat16)
    mixed_rows = jnp.einsum(
        "hgqk,khd->qhgd", weights, value_matrix_rows, preferred_element_type=jnp.float32
    )
    return mixed_rows / jnp.transpose(row_total, (2, 0, 1, 3))


def local(stream, queries, keys, values, out_weight, gains):
    tok_rows = stream.shape[0]
    span_rows = min(tok_rows, WINDOW_LENGTH)
    hop_count = WINDOW_LENGTH // span_rows
    own_tail = (keys[0, tok_rows - span_rows :], values[0, tok_rows - span_rows :])
    pieces = [
        passed_along((own_tail[0], own_tail[1]), "ctx", distance)
        for distance in range(hop_count, 0, -1)
    ]
    key_matrix_rows = jnp.concatenate([piece_pair[0] for piece_pair in pieces] + [keys[0]], axis=0)
    value_matrix_rows = jnp.concatenate(
        [piece_pair[1] for piece_pair in pieces] + [values[0]], axis=0
    )
    ctx_base = lax.axis_index("ctx") * tok_rows
    query_pos = ctx_base + jnp.arange(tok_rows, dtype=jnp.int32)
    key_pos = ctx_base - WINDOW_LENGTH + jnp.arange(WINDOW_LENGTH + tok_rows, dtype=jnp.int32)
    allowed = (
        (key_pos[None, :] >= 0)
        & (key_pos[None, :] <= query_pos[:, None])
        & (key_pos[None, :] > query_pos[:, None] - WINDOW_LENGTH)
    )
    scale_factor = QUERY_SCALAR ** (-0.5)
    heads_per_block = math.gcd(KEY_HEADS, 4)
    query_width = heads_per_block * QUERY_PER_KEY * HEAD_WIDTH
    key_width = heads_per_block * HEAD_WIDTH
    outputs_list = []
    for query_head_group in range(KEY_HEADS // heads_per_block):
        query_cols = queries[
            0, :, query_head_group * query_width : (query_head_group + 1) * query_width
        ].reshape(tok_rows, heads_per_block, QUERY_PER_KEY, HEAD_WIDTH)
        key_cols = key_matrix_rows[
            :, query_head_group * key_width : (query_head_group + 1) * key_width
        ].reshape(WINDOW_LENGTH + tok_rows, heads_per_block, HEAD_WIDTH)
        value_cols = value_matrix_rows[
            :, query_head_group * key_width : (query_head_group + 1) * key_width
        ].reshape(WINDOW_LENGTH + tok_rows, heads_per_block, HEAD_WIDTH)
        mixed_rows = attend_block(query_cols, key_cols, value_cols, allowed, scale_factor)
        outputs_list.append(mixed_rows.reshape(tok_rows, query_width))
    attended = jnp.concatenate(outputs_list, axis=1).astype(jnp.bfloat16)
    projected = jnp.dot(
        attended,
        lax.all_gather(out_weight[0], "ctx", axis=0, tiled=True),
        preferred_element_type=jnp.float32,
    )
    mean_square = jnp.mean(projected * projected, axis=-1, keepdims=True)
    branch = projected * lax.rsqrt(mean_square + norm_eps) * gains[0].astype(jnp.float32)
    section_index = lax.axis_index("section")
    section_count = lax.axis_size("section")
    running = jnp.where(
        section_index == 0, stream.astype(jnp.float32) + branch, jnp.zeros_like(branch)
    )
    for turn_index in range(section_count - 1):
        arrived = passed_along(running.astype(jnp.bfloat16), "section", 1).astype(running.dtype)
        running = jnp.where(section_index == turn_index + 1, arrived + branch, running)
    return running.astype(jnp.bfloat16)[None]


LANES = 128
MESH = pl.DeviceIdType.MESH
CHUNKS = 8
PIECES = 2
FIRST = 2
SECOND = 5
LAST = 8
HOP = 2
TILE = 512
VMEM_GRANT = 60_000_000


def column_tiles(start, stop, width):
    return [(at, min(at + width, stop) - at) for at in range(start, stop, width)]


def fused_kernel(
    sections,
    chunks,
    pieces,
    half,
    gains_hbm,
    stream_ref,
    q_ref,
    k_ref,
    v_ref,
    w_hbm,
    out_ref,
    qbuf,
    kbuf,
    vbuf,
    vturned,
    w_ref,
    gains_ref,
    att,
    pair_out,
    pair_in,
    x1_out,
    y1_out,
    first_in,
    x2_out,
    y2_out,
    second_in,
    own,
    keep_me,
    keep_x,
    keep_y,
    base,
    local_sem,
    key_sem,
    value_sem,
    query_sem,
    sent_sem,
    pair_sem,
    first_sem,
    second_sem,
    chain_sem,
):
    me = lax.axis_index("ctx")
    section = lax.axis_index("section")
    devices, chunk_rows, query_width = qbuf.shape[1:]
    width = w_ref.shape[1]
    rows = chunks * chunk_rows
    piece_rows = chunk_rows // pieces
    quarter, pair_count = devices // 4, devices // 2
    core = me % 2
    across = (me // quarter) % 2
    up = me // pair_count
    flips = (1 - 2 * core, quarter * (1 - 2 * across), pair_count * (1 - 2 * up))

    def peer(flip_core, flip_x, flip_y):
        return me + flips[0] * flip_core + flips[1] * flip_x + flips[2] * flip_y

    sibling, beside, above, diagonal = peer(1, 0, 0), peer(0, 1, 0), peer(0, 0, 1), peer(0, 1, 1)
    has_prev = jnp.minimum(section, 1)
    has_next = jnp.minimum(sections - 1 - section, 1)

    def own_rows(buf):
        return buf.at[pl.ds(pl.multiple_of(me * rows, rows), rows)]

    def head_columns(ref, who, span):
        return ref.at[:, pl.ds(pl.multiple_of(who * span, span), span)]

    w_copy = pltpu.make_async_copy(w_hbm, w_ref, local_sem.at[0])
    w_copy.start()
    gains_copy = pltpu.make_async_copy(gains_hbm, gains_ref, local_sem.at[1])
    gains_copy.start()

    @pl.when(section == 0)
    def _():
        for piece in range(chunks * pieces):
            pltpu.make_async_copy(
                stream_ref.at[pl.ds(piece * piece_rows, piece_rows)],
                base.at[piece],
                chain_sem.at[piece],
            ).start()

    def query_part(who, chunk):
        source = q_ref.at[
            pl.ds(chunk * chunk_rows, chunk_rows),
            pl.ds(pl.multiple_of(who * query_width, query_width), query_width),
        ]
        return source, qbuf.at[chunk, me], sent_sem.at[2], query_sem.at[chunk]

    def blocks_for(who):
        key_block = head_columns(k_ref, who, HEAD_WIDTH), own_rows(kbuf), sent_sem.at[0], key_sem
        value_block = (
            head_columns(v_ref, who, HEAD_WIDTH),
            own_rows(vbuf),
            sent_sem.at[1],
            value_sem.at[me],
        )
        asked = [query_part(who, chunk) for chunk in range(chunks)]
        return [key_block, asked[0], value_block] + asked[1:]

    for source, target, _, landed in blocks_for(me):
        pltpu.make_async_copy(source, target, landed).start()

    order = [(0, 1, 1), (1, 1, 1), (0, 1, 0), (0, 0, 1), (1, 1, 0), (1, 0, 1), (1, 0, 0)]
    barrier = pltpu.get_barrier_semaphore()
    for flip in order:
        pl.semaphore_signal(barrier, inc=1, device_id=(section, peer(*flip)), device_id_type=MESH)

    @pl.when(section > 0)
    def _():
        pl.semaphore_signal(barrier, inc=1, device_id=(section - 1, me), device_id_type=MESH)

    @pl.when(section < sections - 1)
    def _():
        pl.semaphore_signal(barrier, inc=1, device_id=(section + 1, me), device_id_type=MESH)

    pl.semaphore_wait(barrier, len(order) + has_prev + has_next)

    def exchange(who):
        return [
            pltpu.make_async_remote_copy(
                src_ref=source,
                dst_ref=target,
                send_sem=sent,
                recv_sem=landed,
                device_id=(section, who),
                device_id_type=MESH,
            )
            for source, target, sent, landed in blocks_for(who)
        ]

    for wave in zip(*[exchange(peer(*flip)) for flip in order]):
        for copy in wave:
            copy.start()

    def arrive(target, sem):
        pltpu.make_async_copy(target, target, sem).wait()

    narrow = jnp.bfloat16
    factor = QUERY_SCALAR ** (-0.5) * math.log2(math.e)
    group = query_width // HEAD_WIDTH
    asks = devices * group * chunk_rows
    low_asks, low_keys = asks // 2, devices * rows // 2

    def column_positions(chunk):
        lane = lax.broadcasted_iota(jnp.int32, (1, asks), 1)
        block = lane // (group * chunk_rows)
        return block * rows + chunk * chunk_rows + lane % chunk_rows

    def visible(scores, first_key, positions):
        key = lax.broadcasted_iota(jnp.int32, scores.shape, 0) + first_key
        return jnp.where(key <= positions, scores, -jnp.inf)

    def score(key_rows, query_rows):
        return lax.dot_general(
            key_rows, query_rows, (((1,), (1,)), ((), ())), preferred_element_type=jnp.float32
        )

    def turn_values():
        for block in range(devices):
            span = pl.ds(block * rows, rows)
            arrive(vbuf.at[span], value_sem.at[block])
            vturned[:, block * rows : (block + 1) * rows] = vbuf[span].T

    def weigh(chunk):
        arrive(qbuf.at[chunk], query_sem.at[chunk])
        asked = jnp.concatenate(
            [
                qbuf[chunk, block, :, head * HEAD_WIDTH : (head + 1) * HEAD_WIDTH]
                for block in range(devices)
                for head in range(group)
            ],
            axis=0,
        )
        positions = column_positions(chunk)
        early = score(kbuf[:low_keys], asked)
        late = score(kbuf[low_keys:], asked[low_asks:])
        left = visible(early[:, :low_asks], 0, positions[:, :low_asks])
        right = early[:, low_asks:]
        late = visible(late, low_keys, positions[:, low_asks:])
        left_top = jnp.max(left, axis=0, keepdims=True)
        right_top = jnp.maximum(
            jnp.max(right, axis=0, keepdims=True), jnp.max(late, axis=0, keepdims=True)
        )
        left = jnp.exp2((left - left_top) * factor)
        right = jnp.exp2((right - right_top) * factor)
        late = jnp.exp2((late - right_top) * factor)
        left_total = jnp.sum(left, axis=0, keepdims=True)
        right_total = jnp.sum(right, axis=0, keepdims=True) + jnp.sum(late, axis=0, keepdims=True)
        early = jnp.concatenate([left.astype(narrow), right.astype(narrow)], axis=1)
        return early, late.astype(narrow), left_total, right_total

    def mix(chunk, early, late, left_total, right_total):
        mixed = jnp.dot(vturned[:, :low_keys], early, preferred_element_type=jnp.float32)
        mixed_late = jnp.dot(vturned[:, low_keys:], late, preferred_element_type=jnp.float32)
        halves = (
            mixed[:, :low_asks] / left_total,
            (mixed[:, low_asks:] + mixed_late) / right_total,
        )
        for index, part in enumerate(halves):
            turned = part.T.astype(narrow)
            for within in range(devices // 2):
                block = index * (devices // 2) + within
                for head in range(group):
                    start = (within * group + head) * chunk_rows
                    att[
                        block % 2,
                        chunk,
                        block // 2,
                        :,
                        head * HEAD_WIDTH : (head + 1) * HEAD_WIDTH,
                    ] = turned[start : start + chunk_rows]

    def remote(source, target, sent, landed, who):
        return pltpu.make_async_remote_copy(
            src_ref=source,
            dst_ref=target,
            send_sem=sent,
            recv_sem=landed,
            device_id=who,
            device_id_type=MESH,
        )

    def pair_copy(piece):
        return remote(
            pair_out.at[piece],
            pair_in.at[piece],
            sent_sem.at[3],
            pair_sem.at[piece],
            (section, sibling),
        )

    low, high = pl.ds(0, half), pl.ds(half, width - half)

    def x1_copy(piece):
        target = first_in.at[piece, :, :, low]
        return remote(
            x1_out.at[piece], target, sent_sem.at[4], first_sem.at[piece], (section, beside)
        )

    def y1_copy(piece):
        target = first_in.at[piece, :, :, high]
        return remote(
            y1_out.at[piece], target, sent_sem.at[5], first_sem.at[piece], (section, above)
        )

    def x2_copy(piece):
        target = second_in.at[piece, :, high]
        return remote(
            x2_out.at[piece], target, sent_sem.at[6], second_sem.at[piece], (section, beside)
        )

    def y2_copy(piece):
        target = second_in.at[piece, :, low]
        return remote(
            y2_out.at[piece], target, sent_sem.at[7], second_sem.at[piece], (section, above)
        )

    def chain_copy(piece):
        onward = (jnp.minimum(section + 1, sections - 1), me)
        return remote(
            out_ref.at[piece], base.at[piece], sent_sem.at[8], chain_sem.at[piece], onward
        )

    chip_count = pair_count
    places = [who // 2 for who in (beside, diagonal, above, me)]

    def product(chunk):
        theirs = chip_count * chunk_rows
        left = jnp.concatenate(
            [att[1 - core, chunk].reshape(theirs, query_width)]
            + [att[core, chunk, place] for place in places],
            axis=0,
        )
        for at, span in column_tiles(0, width, TILE):
            part = jnp.dot(left, w_ref[:, at : at + span], preferred_element_type=jnp.float32)
            part = part.reshape(2, chip_count, pieces, piece_rows, span)
            for index in range(pieces):
                piece = chunk * pieces + index
                pair_out[piece, :, :, at : at + span] = part[0, :, index].astype(narrow)
                own[piece, :, :, at : at + span] = part[1, :, index]
        for index in range(pieces):
            pair_copy(chunk * pieces + index).start()

    def first_turn(piece):
        arrive(pair_in.at[piece], pair_sem.at[piece])

        def summed(index, at, stop):
            return own[piece, index, :, at:stop] + pair_in[piece, places[index], :, at:stop].astype(
                jnp.float32
            )

        x1_out[piece, 0] = summed(0, 0, half).astype(narrow)
        x1_out[piece, 1] = summed(1, 0, half).astype(narrow)
        x1_copy(piece).start()
        y1_out[piece, 0] = summed(2, half, width).astype(narrow)
        y1_out[piece, 1] = summed(1, half, width).astype(narrow)
        y1_copy(piece).start()
        keep_y[piece] = summed(2, 0, half)
        keep_x[piece] = summed(0, half, width)
        keep_me[piece] = summed(3, 0, width)

    def second_turn(piece):
        arrive(first_in.at[piece], first_sem.at[piece])
        passing = first_in[piece, 1].astype(jnp.float32)
        y2_out[piece] = (keep_y[piece] + passing[:, :half]).astype(narrow)
        y2_copy(piece).start()
        x2_out[piece] = (keep_x[piece] + passing[:, half:]).astype(narrow)
        x2_copy(piece).start()
        keep_me[piece] += first_in[piece, 0].astype(jnp.float32)

    def normalise(piece):
        arrive(second_in.at[piece], second_sem.at[piece])
        full = keep_me[piece] + second_in[piece].astype(jnp.float32)
        squares = jnp.sum(full * full, axis=1, keepdims=True)
        ratio = lax.rsqrt(squares * (1.0 / width) + norm_eps)
        keep_me[piece] = full * ratio * gains_ref[...].astype(jnp.float32)

    def hand_on(piece):
        arrive(base.at[piece], chain_sem.at[piece])
        out_ref[piece] = (base[piece].astype(jnp.float32) + keep_me[piece]).astype(out_ref.dtype)

        @pl.when(section < sections - 1)
        def _():
            chain_copy(piece).start()

    arrive(kbuf, key_sem)
    weights = weigh(0)
    turn_values()
    mix(0, *weights)
    w_copy.wait()
    gains_copy.wait()

    def turn(step, carry):
        chunk = step // pieces
        fresh = step % pieces == 0

        @pl.when(fresh & (chunk > 0) & (chunk < chunks))
        def _():
            mix(chunk, *weigh(chunk))

        @pl.when(fresh & (chunk < chunks))
        def _():
            product(chunk)

        for lag, stage in (
            (FIRST, first_turn),
            (SECOND, second_turn),
            (LAST, normalise),
            (LAST + HOP * section, hand_on),
        ):
            piece = step - lag

            @pl.when((piece >= 0) & (piece < chunks * pieces))
            def _():
                stage(piece)

        return carry

    lax.fori_loop(0, chunks * pieces + LAST + HOP * (sections - 1), turn, 0)

    sent = (
        kbuf.at[pl.ds(0, (devices - 1) * rows)],
        vbuf.at[pl.ds(0, (devices - 1) * rows)],
        qbuf.at[:, pl.ds(0, devices - 1)],
        pair_out,
        x1_out,
        y1_out,
        x2_out,
        y2_out,
    )
    for index, source in enumerate(sent):
        arrive(source, sent_sem.at[index])

    @pl.when(section < sections - 1)
    def _():
        arrive(out_ref, sent_sem.at[len(sent)])


def settle(held_ref, out_ref, sem):
    copy = pltpu.make_async_copy(held_ref, out_ref, sem)
    copy.start()
    copy.wait()


def by_head(sections, chunks, pieces, stream, queries, keys, values, out_weight, gains):
    devices = lax.axis_size("ctx")
    rows, width = stream.shape
    query_width = queries.shape[2] // devices
    chunk_rows = rows // chunks
    piece_rows, count = chunk_rows // pieces, chunks * pieces
    half = (width // LANES + 1) // 2 * LANES
    other = width - half
    chips = devices // 2
    narrow, wide = jnp.bfloat16, jnp.float32
    anywhere = pl.BlockSpec(memory_space=pltpu.HBM)
    in_vmem = pl.BlockSpec(memory_space=pltpu.VMEM)
    dma = pltpu.SemaphoreType.DMA
    out = pl.pallas_call(
        functools.partial(fused_kernel, sections, chunks, pieces, half),
        out_shape=pltpu.VMEM((count, piece_rows, width), narrow),
        in_specs=[anywhere] * 6,
        out_specs=in_vmem,
        scratch_shapes=[
            pltpu.VMEM((chunks, devices, chunk_rows, query_width), narrow),
            pltpu.VMEM((devices * rows, HEAD_WIDTH), narrow),
            pltpu.VMEM((devices * rows, HEAD_WIDTH), narrow),
            pltpu.VMEM((HEAD_WIDTH, devices * rows), narrow),
            pltpu.VMEM(out_weight.shape[1:], narrow),
            pltpu.VMEM(gains.shape, narrow),
            pltpu.VMEM((2, chunks, chips, chunk_rows, query_width), narrow),
            pltpu.VMEM((count, chips, piece_rows, width), narrow),
            pltpu.VMEM((count, chips, piece_rows, width), narrow),
            pltpu.VMEM((count, 2, piece_rows, half), narrow),
            pltpu.VMEM((count, 2, piece_rows, other), narrow),
            pltpu.VMEM((count, 2, piece_rows, width), narrow),
            pltpu.VMEM((count, piece_rows, other), narrow),
            pltpu.VMEM((count, piece_rows, half), narrow),
            pltpu.VMEM((count, piece_rows, width), narrow),
            pltpu.VMEM((count, chips, piece_rows, width), wide),
            pltpu.VMEM((count, piece_rows, width), wide),
            pltpu.VMEM((count, piece_rows, other), wide),
            pltpu.VMEM((count, piece_rows, half), wide),
            pltpu.VMEM((count, piece_rows, width), narrow),
            dma((2,)),
            dma,
            dma((devices,)),
            dma((chunks,)),
            dma((9,)),
            dma((count,)),
            dma((count,)),
            dma((count,)),
            dma((count,)),
        ],
        compiler_params=pltpu.CompilerParams(
            collective_id=0, has_side_effects=True, vmem_limit_bytes=VMEM_GRANT
        ),
    )(gains, stream, queries[0], keys[0], values[0], out_weight[0])
    return pl.pallas_call(
        settle,
        out_shape=jax.ShapeDtypeStruct(out.shape, out.dtype),
        in_specs=[in_vmem],
        out_specs=anywhere,
        scratch_shapes=[dma(())],
        compiler_params=pltpu.CompilerParams(vmem_limit_bytes=2_000_000),
    )(out).reshape(1, rows, width)


def fits_by_head(mesh, rows):
    devices = mesh.shape["ctx"]
    return devices == KEY_HEADS and devices * rows <= WINDOW_LENGTH and devices % 8 == 0


def solution(mesh):
    in_specs = (
        P("ctx", None),
        P("section", "ctx", None),
        P("section", "ctx", None),
        P("section", "ctx", None),
        P("section", "ctx", None),
        P("section", None),
    )
    out_specs = P("section", "ctx", None)
    sections = mesh.shape["section"]

    def step(stream, *rest):
        rows = stream.shape[0]
        if fits_by_head(mesh, rows):
            return by_head(sections, CHUNKS, PIECES, stream, *rest)
        return local(stream, *rest)

    return jax.shard_map(step, mesh=mesh, in_specs=in_specs, out_specs=out_specs, check_vma=False)
```

time: 59.5 us -> 49.4 us (0.83)
  Pallas kernels: 57.3 us -> 49.3 us
  local copies, waits for them, and re-layouts: 1.99 us -> 0 us
    pallas_call x1 -> x2, Pallas kernels: 57.3 us -> 49.3 us  [the longest x1 48.4 us: by_head(): pl.pallas_call(functools.partial(fused_kernel, sections, chunks, pieces,...]
    unnamed x1 -> x0, local copies, waits for them, and re-layouts: 1.99 us -> none
where the time goes in v1:
time: 49.4 us; the launch traced here: 49.3 us
  Pallas kernels  49.3 us (100%)
    pallas_call x1, Pallas kernels, by_head(): pl.pallas_call(functools.partial(fused_kernel, sections, chunks, pieces,...  48.4 us

profile of v1, /device:TPU:24, one launch (start us, length us, event | category | flops | bytes accessed | tf_op | source)
XLA Modules:
  0.0 49.3 jit_solution(4939731325664918090)
XLA Ops:
  0.0 48.4 %shard_map.64.held_ref = bf16[16,8,2688]{2,1,0:T(8,128)(2,1)S(1)} custom-call(bf16[1,2688]{1,0:T(2,128)(2,1)} %gains_hbm.1, bf16[128,2688]{1,0:T(8,128)(2,1)} %stream_ref.1, bf16[128,2048]{1,0:T(8,128)(2,1)} %bitcast.6, bf16[128,1024]{1,0:T(8,128)(2,1)} %bitcast.7, bf16[128,1024]{1,0:T(8,128)(2,1)} %bitcast.8, bf16[256,2688]{1,0:T(8,128)(2,1)} %bitcast.5), custom_call_target="tpu_custom_call" | custom-call | tf_op jit(solution)/shard_map/pallas_call | solution.py:515
  48.4 0.9 %shard_map.65 = bf16[16,8,2688]{2,1,0:T(8,128)(2,1)} custom-call(bf16[16,8,2688]{2,1,0:T(8,128)(2,1)S(1)} %shard_map.64.held_ref), custom_call_target="tpu_custom_call" | custom-call | tf_op jit(solution)/shard_map/pallas_call | solution.py:555

commit v2 on v1

--- a/solution.py
+++ b/solution.py
@@ -103,9 +103,9 @@
 MESH = pl.DeviceIdType.MESH
 CHUNKS = 8
 PIECES = 2
-FIRST = 2
-SECOND = 5
-LAST = 8
+FIRST = 1
+SECOND = 4
+LAST = 7
 HOP = 2
 TILE = 512
 VMEM_GRANT = 60_000_000
@@ -136,11 +136,13 @@
     att,
     pair_out,
     pair_in,
-    x1_out,
-    y1_out,
+    far_x,
+    far_y,
     first_in,
-    x2_out,
-    y2_out,
+    near_x,
+    near_y,
+    onward_x,
+    onward_y,
     second_in,
     own,
     keep_me,
@@ -209,7 +211,7 @@
             head_columns(v_ref, who, HEAD_WIDTH),
             own_rows(vbuf),
             sent_sem.at[1],
-            value_sem.at[me],
+            value_sem.at[me // pair_count],
         )
         asked = [query_part(who, chunk) for chunk in range(chunks)]
         return [key_block, asked[0], value_block] + asked[1:]
@@ -273,10 +275,10 @@
         )
 
     def turn_values():
-        for block in range(devices):
-            span = pl.ds(block * rows, rows)
-            arrive(vbuf.at[span], value_sem.at[block])
-            vturned[:, block * rows : (block + 1) * rows] = vbuf[span].T
+        for side in range(2):
+            span = pl.ds(side * low_keys, low_keys)
+            arrive(vbuf.at[span], value_sem.at[side])
+            vturned[:, side * low_keys : (side + 1) * low_keys] = vbuf[span].T
 
     def weigh(chunk):
         arrive(qbuf.at[chunk], query_sem.at[chunk])
@@ -337,45 +339,35 @@
             device_id_type=MESH,
         )
 
-    def pair_copy(piece):
+    def pair_copy(chunk):
+        span = pl.ds(chunk * pieces, pieces)
+        landed = pair_sem.at[chunk % pair_sem.shape[0]]
         return remote(
-            pair_out.at[piece],
-            pair_in.at[piece],
-            sent_sem.at[3],
-            pair_sem.at[piece],
-            (section, sibling),
+            pair_out.at[span], pair_in.at[span], sent_sem.at[3], landed, (section, sibling)
         )
 
     low, high = pl.ds(0, half), pl.ds(half, width - half)
 
-    def x1_copy(piece):
-        target = first_in.at[piece, :, :, low]
-        return remote(
-            x1_out.at[piece], target, sent_sem.at[4], first_sem.at[piece], (section, beside)
-        )
-
-    def y1_copy(piece):
-        target = first_in.at[piece, :, :, high]
-        return remote(
-            y1_out.at[piece], target, sent_sem.at[5], first_sem.at[piece], (section, above)
-        )
-
-    def x2_copy(piece):
-        target = second_in.at[piece, :, high]
-        return remote(
-            x2_out.at[piece], target, sent_sem.at[6], second_sem.at[piece], (section, beside)
-        )
-
-    def y2_copy(piece):
-        target = second_in.at[piece, :, low]
-        return remote(
-            y2_out.at[piece], target, sent_sem.at[7], second_sem.at[piece], (section, above)
-        )
+    def first_copies(piece):
+        landed = first_sem.at[piece % first_sem.shape[0]]
+        for source, columns, who in ((far_x, low, beside), (far_y, high, above)):
+            target = first_in.at[piece, :, columns]
+            remote(source.at[piece], target, sent_sem.at[4], landed, (section, who)).start()
+
+    def second_copies(piece, which):
+        landed = second_sem.at[piece]
+        sends = (
+            ((near_x, low, beside), (near_y, high, above)),
+            ((onward_y, low, above), (onward_x, high, beside)),
+        )
+        for source, columns, who in sends[which]:
+            target = second_in.at[piece, which, :, columns]
+            remote(source.at[piece], target, sent_sem.at[5], landed, (section, who)).start()
 
     def chain_copy(piece):
         onward = (jnp.minimum(section + 1, sections - 1), me)
         return remote(
-            out_ref.at[piece], base.at[piece], sent_sem.at[8], chain_sem.at[piece], onward
+            out_ref.at[piece], base.at[piece], sent_sem.at[6], chain_sem.at[piece], onward
         )
 
     chip_count = pair_count
@@ -395,39 +387,42 @@
                 piece = chunk * pieces + index
                 pair_out[piece, :, :, at : at + span] = part[0, :, index].astype(narrow)
                 own[piece, :, :, at : at + span] = part[1, :, index]
-        for index in range(pieces):
-            pair_copy(chunk * pieces + index).start()
+        pair_copy(chunk).start()
 
     def first_turn(piece):
-        arrive(pair_in.at[piece], pair_sem.at[piece])
+        chunk = piece // pieces
+
+        @pl.when(piece % pieces == 0)
+        def _():
+            span = pl.ds(chunk * pieces, pieces)
+            arrive(pair_in.at[span], pair_sem.at[chunk % pair_sem.shape[0]])
 
         def summed(index, at, stop):
             return own[piece, index, :, at:stop] + pair_in[piece, places[index], :, at:stop].astype(
                 jnp.float32
             )
 
-        x1_out[piece, 0] = summed(0, 0, half).astype(narrow)
-        x1_out[piece, 1] = summed(1, 0, half).astype(narrow)
-        x1_copy(piece).start()
-        y1_out[piece, 0] = summed(2, half, width).astype(narrow)
-        y1_out[piece, 1] = summed(1, half, width).astype(narrow)
-        y1_copy(piece).start()
+        far_x[piece] = summed(1, 0, half).astype(narrow)
+        far_y[piece] = summed(1, half, width).astype(narrow)
+        first_copies(piece)
+        near_x[piece] = summed(0, 0, half).astype(narrow)
+        near_y[piece] = summed(2, half, width).astype(narrow)
+        second_copies(piece, 0)
         keep_y[piece] = summed(2, 0, half)
         keep_x[piece] = summed(0, half, width)
         keep_me[piece] = summed(3, 0, width)
 
     def second_turn(piece):
-        arrive(first_in.at[piece], first_sem.at[piece])
-        passing = first_in[piece, 1].astype(jnp.float32)
-        y2_out[piece] = (keep_y[piece] + passing[:, :half]).astype(narrow)
-        y2_copy(piece).start()
-        x2_out[piece] = (keep_x[piece] + passing[:, half:]).astype(narrow)
-        x2_copy(piece).start()
-        keep_me[piece] += first_in[piece, 0].astype(jnp.float32)
+        arrive(first_in.at[piece], first_sem.at[piece % first_sem.shape[0]])
+        passing = first_in[piece].astype(jnp.float32)
+        onward_y[piece] = (keep_y[piece] + passing[:, :half]).astype(narrow)
+        onward_x[piece] = (keep_x[piece] + passing[:, half:]).astype(narrow)
+        second_copies(piece, 1)
 
     def normalise(piece):
         arrive(second_in.at[piece], second_sem.at[piece])
-        full = keep_me[piece] + second_in[piece].astype(jnp.float32)
+        received = second_in[piece].astype(jnp.float32)
+        full = keep_me[piece] + received[0] + received[1]
         squares = jnp.sum(full * full, axis=1, keepdims=True)
         ratio = lax.rsqrt(squares * (1.0 / width) + norm_eps)
         keep_me[piece] = full * ratio * gains_ref[...].astype(jnp.float32)
@@ -446,31 +441,27 @@
     mix(0, *weights)
     w_copy.wait()
     gains_copy.wait()
+    product(0)
 
     def turn(step, carry):
-        chunk = step // pieces
-        fresh = step % pieces == 0
-
-        @pl.when(fresh & (chunk > 0) & (chunk < chunks))
-        def _():
-            mix(chunk, *weigh(chunk))
-
-        @pl.when(fresh & (chunk < chunks))
-        def _():
-            product(chunk)
-
-        for lag, stage in (
-            (FIRST, first_turn),
-            (SECOND, second_turn),
-            (LAST, normalise),
-            (LAST + HOP * section, hand_on),
-        ):
+        def staged(lag, stage):
             piece = step - lag
 
             @pl.when((piece >= 0) & (piece < chunks * pieces))
             def _():
                 stage(piece)
 
+        staged(FIRST, first_turn)
+        chunk = step // pieces + 1
+
+        @pl.when((step % pieces == 0) & (chunk < chunks))
+        def _():
+            mix(chunk, *weigh(chunk))
+            product(chunk)
+
+        staged(SECOND, second_turn)
+        staged(LAST, normalise)
+        staged(LAST + HOP * section, hand_on)
         return carry
 
     lax.fori_loop(0, chunks * pieces + LAST + HOP * (sections - 1), turn, 0)
@@ -480,10 +471,8 @@
         vbuf.at[pl.ds(0, (devices - 1) * rows)],
         qbuf.at[:, pl.ds(0, devices - 1)],
         pair_out,
-        x1_out,
-        y1_out,
-        x2_out,
-        y2_out,
+        first_in,
+        second_in,
     )
     for index, source in enumerate(sent):
         arrive(source, sent_sem.at[index])
@@ -527,12 +516,14 @@
             pltpu.VMEM((2, chunks, chips, chunk_rows, query_width), narrow),
             pltpu.VMEM((count, chips, piece_rows, width), narrow),
             pltpu.VMEM((count, chips, piece_rows, width), narrow),
-            pltpu.VMEM((count, 2, piece_rows, half), narrow),
-            pltpu.VMEM((count, 2, piece_rows, other), narrow),
-            pltpu.VMEM((count, 2, piece_rows, width), narrow),
+            pltpu.VMEM((count, piece_rows, half), narrow),
+            pltpu.VMEM((count, piece_rows, other), narrow),
+            pltpu.VMEM((count, piece_rows, width), narrow),
+            pltpu.VMEM((count, piece_rows, half), narrow),
+            pltpu.VMEM((count, piece_rows, other), narrow),
             pltpu.VMEM((count, piece_rows, other), narrow),
             pltpu.VMEM((count, piece_rows, half), narrow),
-            pltpu.VMEM((count, piece_rows, width), narrow),
+            pltpu.VMEM((count, 2, piece_rows, width), narrow),
             pltpu.VMEM((count, chips, piece_rows, width), wide),
             pltpu.VMEM((count, piece_rows, width), wide),
             pltpu.VMEM((count, piece_rows, other), wide),
@@ -540,11 +531,11 @@
             pltpu.VMEM((count, piece_rows, width), narrow),
             dma((2,)),
             dma,
-            dma((devices,)),
+            dma((2,)),
             dma((chunks,)),
-            dma((9,)),
-            dma((count,)),
-            dma((count,)),
+            dma((7,)),
+            dma((min(chunks, 4),)),
+            dma((min(count, 8),)),
             dma((count,)),
             dma((count,)),
         ],

time: 49.4 us -> 48.5 us (0.982)
  Pallas kernels: 49.3 us -> 48.4 us
    pallas_call x1, Pallas kernels: 48.4 us -> 47.5 us  [by_head(): pl.pallas_call(functools.partial(fused_kernel, sections, chunks, pieces,...]
where the time goes in v2:
time: 48.5 us; the launch traced here: 48.4 us
  Pallas kernels  48.4 us (100%)
    pallas_call x1, Pallas kernels, by_head(): pl.pallas_call(functools.partial(fused_kernel, sections, chunks, pieces,...  47.5 us

profile of v2, /device:TPU:24, one launch (start us, length us, event | category | flops | bytes accessed | tf_op | source)
XLA Modules:
  0.0 48.4 jit_solution(3547992811241077948)
XLA Ops:
  0.0 47.5 %shard_map.64.held_ref = bf16[16,8,2688]{2,1,0:T(8,128)(2,1)S(1)} custom-call(bf16[1,2688]{1,0:T(2,128)(2,1)} %gains_hbm.1, bf16[128,2688]{1,0:T(8,128)(2,1)} %stream_ref.1, bf16[128,2048]{1,0:T(8,128)(2,1)} %bitcast.6, bf16[128,1024]{1,0:T(8,128)(2,1)} %bitcast.7, bf16[128,1024]{1,0:T(8,128)(2,1)} %bitcast.8, bf16[256,2688]{1,0:T(8,128)(2,1)} %bitcast.5), custom_call_target="tpu_custom_call" | custom-call | tf_op jit(solution)/shard_map/pallas_call | solution.py:504
  47.5 0.9 %shard_map.65 = bf16[16,8,2688]{2,1,0:T(8,128)(2,1)} custom-call(bf16[16,8,2688]{2,1,0:T(8,128)(2,1)S(1)} %shard_map.64.held_ref), custom_call_target="tpu_custom_call" | custom-call | tf_op jit(solution)/shard_map/pallas_call | solution.py:546

commit v3 on v2

--- a/solution.py
+++ b/solution.py
@@ -107,6 +107,7 @@
 SECOND = 4
 LAST = 7
 HOP = 2
+TAIL = 4
 TILE = 512
 VMEM_GRANT = 60_000_000
 
@@ -136,18 +137,14 @@
     att,
     pair_out,
     pair_in,
-    far_x,
-    far_y,
+    far,
     first_in,
-    near_x,
-    near_y,
-    onward_x,
-    onward_y,
+    near,
+    onward,
     second_in,
     own,
     keep_me,
-    keep_x,
-    keep_y,
+    keep,
     base,
     local_sem,
     key_sem,
@@ -184,6 +181,14 @@
     def head_columns(ref, who, span):
         return ref.at[:, pl.ds(pl.multiple_of(who * span, span), span)]
 
+    tail_start = chunks * pieces - TAIL
+    sides = ((0, half), (half, width))
+
+    def hand_parts(late, piece):
+        if late:
+            return (sides[0], piece), (sides[1], piece + TAIL)
+        return (((0, width), piece),)
+
     w_copy = pltpu.make_async_copy(w_hbm, w_ref, local_sem.at[0])
     w_copy.start()
     gains_copy = pltpu.make_async_copy(gains_hbm, gains_ref, local_sem.at[1])
@@ -192,11 +197,13 @@
     @pl.when(section == 0)
     def _():
         for piece in range(chunks * pieces):
-            pltpu.make_async_copy(
-                stream_ref.at[pl.ds(piece * piece_rows, piece_rows)],
-                base.at[piece],
-                chain_sem.at[piece],
-            ).start()
+            for (at, stop), landed in hand_parts(piece >= tail_start, piece):
+                columns = pl.ds(at, stop - at)
+                pltpu.make_async_copy(
+                    stream_ref.at[pl.ds(piece * piece_rows, piece_rows), columns],
+                    base.at[piece, :, columns],
+                    chain_sem.at[landed],
+                ).start()
 
     def query_part(who, chunk):
         source = q_ref.at[
@@ -346,29 +353,35 @@
             pair_out.at[span], pair_in.at[span], sent_sem.at[3], landed, (section, sibling)
         )
 
-    low, high = pl.ds(0, half), pl.ds(half, width - half)
+    def for_each_way(piece, send):
+        for odd in range(2):
+
+            @pl.when(piece % 2 == odd)
+            def _():
+                send(sides[odd], sides[1 - odd])
 
     def first_copies(piece):
         landed = first_sem.at[piece % first_sem.shape[0]]
-        for source, columns, who in ((far_x, low, beside), (far_y, high, above)):
-            target = first_in.at[piece, :, columns]
-            remote(source.at[piece], target, sent_sem.at[4], landed, (section, who)).start()
-
-    def second_copies(piece, which):
-        landed = second_sem.at[piece]
-        sends = (
-            ((near_x, low, beside), (near_y, high, above)),
-            ((onward_y, low, above), (onward_x, high, beside)),
-        )
-        for source, columns, who in sends[which]:
-            target = second_in.at[piece, which, :, columns]
-            remote(source.at[piece], target, sent_sem.at[5], landed, (section, who)).start()
-
-    def chain_copy(piece):
-        onward = (jnp.minimum(section + 1, sections - 1), me)
-        return remote(
-            out_ref.at[piece], base.at[piece], sent_sem.at[6], chain_sem.at[piece], onward
-        )
+
+        def send(by_x, by_y):
+            for (at, stop), who in ((by_x, beside), (by_y, above)):
+                part = piece, slice(None), pl.ds(at, stop - at)
+                remote(
+                    far.at[part], first_in.at[part], sent_sem.at[4], landed, (section, who)
+                ).start()
+
+        for_each_way(piece, send)
+
+    def second_copies(piece, which, by_x, by_y):
+        for (at, stop), who in ((by_x, beside), (by_y, above)):
+            columns = pl.ds(at, stop - at)
+            remote(
+                (near, onward)[which].at[piece, :, columns],
+                second_in.at[piece, which, :, columns],
+                sent_sem.at[5],
+                second_sem.at[piece],
+                (section, who),
+            ).start()
 
     chip_count = pair_count
     places = [who // 2 for who in (beside, diagonal, above, me)]
@@ -402,22 +415,23 @@
                 jnp.float32
             )
 
-        far_x[piece] = summed(1, 0, half).astype(narrow)
-        far_y[piece] = summed(1, half, width).astype(narrow)
+        far[piece] = summed(1, 0, width).astype(narrow)
         first_copies(piece)
-        near_x[piece] = summed(0, 0, half).astype(narrow)
-        near_y[piece] = summed(2, half, width).astype(narrow)
-        second_copies(piece, 0)
-        keep_y[piece] = summed(2, 0, half)
-        keep_x[piece] = summed(0, half, width)
+
+        def send(by_x, by_y):
+            near[piece, :, by_x[0] : by_x[1]] = summed(0, *by_x).astype(narrow)
+            near[piece, :, by_y[0] : by_y[1]] = summed(2, *by_y).astype(narrow)
+            second_copies(piece, 0, by_x, by_y)
+            keep[piece, :, by_x[0] : by_x[1]] = summed(2, *by_x)
+            keep[piece, :, by_y[0] : by_y[1]] = summed(0, *by_y)
+
+        for_each_way(piece, send)
         keep_me[piece] = summed(3, 0, width)
 
     def second_turn(piece):
         arrive(first_in.at[piece], first_sem.at[piece % first_sem.shape[0]])
-        passing = first_in[piece].astype(jnp.float32)
-        onward_y[piece] = (keep_y[piece] + passing[:, :half]).astype(narrow)
-        onward_x[piece] = (keep_x[piece] + passing[:, half:]).astype(narrow)
-        second_copies(piece, 1)
+        onward[piece] = (keep[piece] + first_in[piece].astype(jnp.float32)).astype(narrow)
+        for_each_way(piece, lambda by_x, by_y: second_copies(piece, 1, by_y, by_x))
 
     def normalise(piece):
         arrive(second_in.at[piece], second_sem.at[piece])
@@ -427,13 +441,33 @@
         ratio = lax.rsqrt(squares * (1.0 / width) + norm_eps)
         keep_me[piece] = full * ratio * gains_ref[...].astype(jnp.float32)
 
+    onward_device = (jnp.minimum(section + 1, sections - 1), me)
+
+    def hand_parts_on(late, piece):
+        for (at, stop), landed in hand_parts(late, piece):
+            part = piece, slice(None), pl.ds(at, stop - at)
+            arrive(base.at[part], chain_sem.at[landed])
+            added = base[piece, :, at:stop].astype(jnp.float32) + keep_me[piece, :, at:stop]
+            out_ref[piece, :, at:stop] = added.astype(out_ref.dtype)
+
+            @pl.when(section < sections - 1)
+            def _():
+                remote(
+                    out_ref.at[part],
+                    base.at[part],
+                    sent_sem.at[6],
+                    chain_sem.at[landed],
+                    onward_device,
+                ).start()
+
     def hand_on(piece):
-        arrive(base.at[piece], chain_sem.at[piece])
-        out_ref[piece] = (base[piece].astype(jnp.float32) + keep_me[piece]).astype(out_ref.dtype)
-
-        @pl.when(section < sections - 1)
+        @pl.when(piece < tail_start)
         def _():
-            chain_copy(piece).start()
+            hand_parts_on(False, piece)
+
+        @pl.when(piece >= tail_start)
+        def _():
+            hand_parts_on(True, piece)
 
     arrive(kbuf, key_sem)
     weights = weigh(0)
@@ -495,7 +529,6 @@
     chunk_rows = rows // chunks
     piece_rows, count = chunk_rows // pieces, chunks * pieces
     half = (width // LANES + 1) // 2 * LANES
-    other = width - half
     chips = devices // 2
     narrow, wide = jnp.bfloat16, jnp.float32
     anywhere = pl.BlockSpec(memory_space=pltpu.HBM)
@@ -516,18 +549,14 @@
             pltpu.VMEM((2, chunks, chips, chunk_rows, query_width), narrow),
             pltpu.VMEM((count, chips, piece_rows, width), narrow),
             pltpu.VMEM((count, chips, piece_rows, width), narrow),
-            pltpu.VMEM((count, piece_rows, half), narrow),
-            pltpu.VMEM((count, piece_rows, other), narrow),
             pltpu.VMEM((count, piece_rows, width), narrow),
-            pltpu.VMEM((count, piece_rows, half), narrow),
-            pltpu.VMEM((count, piece_rows, other), narrow),
-            pltpu.VMEM((count, piece_rows, other), narrow),
-            pltpu.VMEM((count, piece_rows, half), narrow),
+            pltpu.VMEM((count, piece_rows, width), narrow),
+            pltpu.VMEM((count, piece_rows, width), narrow),
+            pltpu.VMEM((count, piece_rows, width), narrow),
             pltpu.VMEM((count, 2, piece_rows, width), narrow),
             pltpu.VMEM((count, chips, piece_rows, width), wide),
             pltpu.VMEM((count, piece_rows, width), wide),
-            pltpu.VMEM((count, piece_rows, other), wide),
-            pltpu.VMEM((count, piece_rows, half), wide),
+            pltpu.VMEM((count, piece_rows, width), wide),
             pltpu.VMEM((count, piece_rows, width), narrow),
             dma((2,)),
             dma,
@@ -537,7 +566,7 @@
             dma((min(chunks, 4),)),
             dma((min(count, 8),)),
             dma((count,)),
-            dma((count,)),
+            dma((count + TAIL,)),
         ],
         compiler_params=pltpu.CompilerParams(
             collective_id=0, has_side_effects=True, vmem_limit_bytes=VMEM_GRANT

time: 48.5 us -> 47.7 us (0.984)
  Pallas kernels: 48.4 us -> 47.6 us
    pallas_call x1, Pallas kernels: 47.5 us -> 46.7 us  [by_head(): pl.pallas_call(functools.partial(fused_kernel, sections, chunks, pieces,...]
where the time goes in v3:
time: 47.7 us; the launch traced here: 47.6 us
  Pallas kernels  47.6 us (100%)
    pallas_call x1, Pallas kernels, by_head(): pl.pallas_call(functools.partial(fused_kernel, sections, chunks, pieces,...  46.7 us

profile of v3, /device:TPU:24, one launch (start us, length us, event | category | flops | bytes accessed | tf_op | source)
XLA Modules:
  0.0 47.6 jit_solution(13694309574962235571)
XLA Ops:
  0.0 46.7 %shard_map.64.held_ref = bf16[16,8,2688]{2,1,0:T(8,128)(2,1)S(1)} custom-call(bf16[1,2688]{1,0:T(2,128)(2,1)} %gains_hbm.1, bf16[128,2688]{1,0:T(8,128)(2,1)} %stream_ref.1, bf16[128,2048]{1,0:T(8,128)(2,1)} %bitcast.6, bf16[128,1024]{1,0:T(8,128)(2,1)} %bitcast.7, bf16[128,1024]{1,0:T(8,128)(2,1)} %bitcast.8, bf16[256,2688]{1,0:T(8,128)(2,1)} %bitcast.5), custom_call_target="tpu_custom_call" | custom-call | tf_op jit(solution)/shard_map/pallas_call | solution.py:537
  46.7 0.9 %shard_map.65 = bf16[16,8,2688]{2,1,0:T(8,128)(2,1)} custom-call(bf16[16,8,2688]{2,1,0:T(8,128)(2,1)S(1)} %shard_map.64.held_ref), custom_call_target="tpu_custom_call" | custom-call | tf_op jit(solution)/shard_map/pallas_call | solution.py:575

commit v4 on v3

--- a/solution.py
+++ b/solution.py
@@ -104,8 +104,9 @@
 CHUNKS = 8
 PIECES = 2
 FIRST = 1
-SECOND = 4
-LAST = 7
+NEAR = 2
+SECOND = 3
+LAST = 6
 HOP = 2
 TAIL = 4
 TILE = 512
@@ -402,7 +403,12 @@
                 own[piece, :, :, at : at + span] = part[1, :, index]
         pair_copy(chunk).start()
 
-    def first_turn(piece):
+    def summed(piece, index, at, stop):
+        return own[piece, index, :, at:stop] + pair_in[piece, places[index], :, at:stop].astype(
+            jnp.float32
+        )
+
+    def send_far(piece):
         chunk = piece // pieces
 
         @pl.when(piece % pieces == 0)
@@ -410,23 +416,19 @@
             span = pl.ds(chunk * pieces, pieces)
             arrive(pair_in.at[span], pair_sem.at[chunk % pair_sem.shape[0]])
 
-        def summed(index, at, stop):
-            return own[piece, index, :, at:stop] + pair_in[piece, places[index], :, at:stop].astype(
-                jnp.float32
-            )
-
-        far[piece] = summed(1, 0, width).astype(narrow)
+        far[piece] = summed(piece, 1, 0, width).astype(narrow)
         first_copies(piece)
 
+    def send_near(piece):
         def send(by_x, by_y):
-            near[piece, :, by_x[0] : by_x[1]] = summed(0, *by_x).astype(narrow)
-            near[piece, :, by_y[0] : by_y[1]] = summed(2, *by_y).astype(narrow)
+            near[piece, :, by_x[0] : by_x[1]] = summed(piece, 0, *by_x).astype(narrow)
+            near[piece, :, by_y[0] : by_y[1]] = summed(piece, 2, *by_y).astype(narrow)
             second_copies(piece, 0, by_x, by_y)
-            keep[piece, :, by_x[0] : by_x[1]] = summed(2, *by_x)
-            keep[piece, :, by_y[0] : by_y[1]] = summed(0, *by_y)
+            keep[piece, :, by_x[0] : by_x[1]] = summed(piece, 2, *by_x)
+            keep[piece, :, by_y[0] : by_y[1]] = summed(piece, 0, *by_y)
 
         for_each_way(piece, send)
-        keep_me[piece] = summed(3, 0, width)
+        keep_me[piece] = summed(piece, 3, 0, width)
 
     def second_turn(piece):
         arrive(first_in.at[piece], first_sem.at[piece % first_sem.shape[0]])
@@ -477,6 +479,8 @@
     gains_copy.wait()
     product(0)
 
+    count = chunks * pieces
+
     def turn(step, carry):
         def staged(lag, stage):
             piece = step - lag
@@ -485,7 +489,14 @@
             def _():
                 stage(piece)
 
-        staged(FIRST, first_turn)
+        ahead = step - FIRST
+
+        @pl.when((ahead % pieces == 0) & (ahead >= 0) & (ahead < count))
+        def _():
+            for index in range(pieces):
+                send_far(ahead + index)
+
+        staged(NEAR, send_near)
         chunk = step // pieces + 1
 
         @pl.when((step % pieces == 0) & (chunk < chunks))

time: 47.7 us -> 47.3 us (level)
  Pallas kernels: 47.6 us -> 47.1 us
where the time goes in v4:
time: 47.3 us; the launch traced here: 47.2 us
  Pallas kernels  47.1 us (100%)
    pallas_call x1, Pallas kernels, by_head(): pl.pallas_call(functools.partial(fused_kernel, sections, chunks, pieces,...  46.3 us

profile of v4, /device:TPU:24, one launch (start us, length us, event | category | flops | bytes accessed | tf_op | source)
XLA Modules:
  0.0 47.2 jit_solution(4164881383294442757)
XLA Ops:
  0.0 46.3 %shard_map.64.held_ref = bf16[16,8,2688]{2,1,0:T(8,128)(2,1)S(1)} custom-call(bf16[1,2688]{1,0:T(2,128)(2,1)} %gains_hbm.1, bf16[128,2688]{1,0:T(8,128)(2,1)} %stream_ref.1, bf16[128,2048]{1,0:T(8,128)(2,1)} %bitcast.6, bf16[128,1024]{1,0:T(8,128)(2,1)} %bitcast.7, bf16[128,1024]{1,0:T(8,128)(2,1)} %bitcast.8, bf16[256,2688]{1,0:T(8,128)(2,1)} %bitcast.5), custom_call_target="tpu_custom_call" | custom-call | tf_op jit(solution)/shard_map/pallas_call | solution.py:548
  46.3 0.9 %shard_map.65 = bf16[16,8,2688]{2,1,0:T(8,128)(2,1)} custom-call(bf16[16,8,2688]{2,1,0:T(8,128)(2,1)S(1)} %shard_map.64.held_ref), custom_call_target="tpu_custom_call" | custom-call | tf_op jit(solution)/shard_map/pallas_call | solution.py:586

commit v5 on v4

--- a/solution.py
+++ b/solution.py
@@ -104,10 +104,10 @@
 CHUNKS = 8
 PIECES = 2
 FIRST = 1
-NEAR = 2
+NEAR = 3
 SECOND = 3
 LAST = 6
-HOP = 2
+HOP = 1
 TAIL = 4
 TILE = 512
 VMEM_GRANT = 60_000_000
@@ -478,6 +478,8 @@
     w_copy.wait()
     gains_copy.wait()
     product(0)
+    mix(1, *weigh(1))
+    product(1)
 
     count = chunks * pieces
 
@@ -497,9 +499,9 @@
                 send_far(ahead + index)
 
         staged(NEAR, send_near)
-        chunk = step // pieces + 1
-
-        @pl.when((step % pieces == 0) & (chunk < chunks))
+        chunk = step // pieces + 2
+
+        @pl.when((step % pieces == pieces - 1) & (chunk < chunks))
         def _():
             mix(chunk, *weigh(chunk))
             product(chunk)

time: 47.3 us -> 46.8 us (0.989)
  Pallas kernels: 47.1 us -> 46.6 us
    pallas_call x1, Pallas kernels: 46.3 us -> 45.8 us  [by_head(): pl.pallas_call(functools.partial(fused_kernel, sections, chunks, pieces,...]
where the time goes in v5:
time: 46.8 us; the launch traced here: 46.6 us
  Pallas kernels  46.6 us (100%)
    pallas_call x1, Pallas kernels, by_head(): pl.pallas_call(functools.partial(fused_kernel, sections, chunks, pieces,...  45.8 us

profile of v5, /device:TPU:24, one launch (start us, length us, event | category | flops | bytes accessed | tf_op | source)
XLA Modules:
  0.0 46.6 jit_solution(6920178766911596403)
XLA Ops:
  0.0 45.8 %shard_map.64.held_ref = bf16[16,8,2688]{2,1,0:T(8,128)(2,1)S(1)} custom-call(bf16[1,2688]{1,0:T(2,128)(2,1)} %gains_hbm.1, bf16[128,2688]{1,0:T(8,128)(2,1)} %stream_ref.1, bf16[128,2048]{1,0:T(8,128)(2,1)} %bitcast.6, bf16[128,1024]{1,0:T(8,128)(2,1)} %bitcast.7, bf16[128,1024]{1,0:T(8,128)(2,1)} %bitcast.8, bf16[256,2688]{1,0:T(8,128)(2,1)} %bitcast.5), custom_call_target="tpu_custom_call" | custom-call | tf_op jit(solution)/shard_map/pallas_call | solution.py:550
  45.8 0.9 %shard_map.65 = bf16[16,8,2688]{2,1,0:T(8,128)(2,1)} custom-call(bf16[16,8,2688]{2,1,0:T(8,128)(2,1)S(1)} %shard_map.64.held_ref), custom_call_target="tpu_custom_call" | custom-call | tf_op jit(solution)/shard_map/pallas_call | solution.py:588

commit v6 on v5

--- a/solution.py
+++ b/solution.py
@@ -108,7 +108,8 @@
 SECOND = 3
 LAST = 6
 HOP = 1
-TAIL = 4
+TAIL = 5
+HAND = 3
 TILE = 512
 VMEM_GRANT = 60_000_000
 
@@ -187,7 +188,10 @@
 
     def hand_parts(late, piece):
         if late:
-            return (sides[0], piece), (sides[1], piece + TAIL)
+            edges = [width // LANES * part // HAND * LANES for part in range(HAND + 1)]
+            return tuple(
+                (edges[part : part + 2], piece + part * TAIL) for part in range(HAND)
+            )
         return (((0, width), piece),)
 
     w_copy = pltpu.make_async_copy(w_hbm, w_ref, local_sem.at[0])
@@ -380,7 +384,7 @@
                 (near, onward)[which].at[piece, :, columns],
                 second_in.at[piece, which, :, columns],
                 sent_sem.at[5],
-                second_sem.at[piece],
+                second_sem.at[piece % second_sem.shape[0]],
                 (section, who),
             ).start()
 
@@ -436,7 +440,7 @@
         for_each_way(piece, lambda by_x, by_y: second_copies(piece, 1, by_y, by_x))
 
     def normalise(piece):
-        arrive(second_in.at[piece], second_sem.at[piece])
+        arrive(second_in.at[piece], second_sem.at[piece % second_sem.shape[0]])
         received = second_in[piece].astype(jnp.float32)
         full = keep_me[piece] + received[0] + received[1]
         squares = jnp.sum(full * full, axis=1, keepdims=True)
@@ -578,8 +582,8 @@
             dma((7,)),
             dma((min(chunks, 4),)),
             dma((min(count, 8),)),
-            dma((count,)),
-            dma((count + TAIL,)),
+            dma((min(count, 12),)),
+            dma((count + (HAND - 1) * TAIL,)),
         ],
         compiler_params=pltpu.CompilerParams(
             collective_id=0, has_side_effects=True, vmem_limit_bytes=VMEM_GRANT

time: 46.8 us -> 46.6 us (level)
  no operation moved by 1% of the time
where the time goes in v6:
time: 46.6 us; the launch traced here: 46.5 us
  Pallas kernels  46.5 us (100%)
    pallas_call x1, Pallas kernels, by_head(): pl.pallas_call(functools.partial(fused_kernel, sections, chunks, pieces,...  45.6 us

profile of v6, /device:TPU:24, one launch (start us, length us, event | category | flops | bytes accessed | tf_op | source)
XLA Modules:
  0.0 46.5 jit_solution(4583508718057891522)
XLA Ops:
  0.0 45.6 %shard_map.64.held_ref = bf16[16,8,2688]{2,1,0:T(8,128)(2,1)S(1)} custom-call(bf16[1,2688]{1,0:T(2,128)(2,1)} %gains_hbm.1, bf16[128,2688]{1,0:T(8,128)(2,1)} %stream_ref.1, bf16[128,2048]{1,0:T(8,128)(2,1)} %bitcast.6, bf16[128,1024]{1,0:T(8,128)(2,1)} %bitcast.7, bf16[128,1024]{1,0:T(8,128)(2,1)} %bitcast.8, bf16[256,2688]{1,0:T(8,128)(2,1)} %bitcast.5), custom_call_target="tpu_custom_call" | custom-call | tf_op jit(solution)/shard_map/pallas_call | solution.py:554
  45.6 0.9 %shard_map.65 = bf16[16,8,2688]{2,1,0:T(8,128)(2,1)} custom-call(bf16[16,8,2688]{2,1,0:T(8,128)(2,1)S(1)} %shard_map.64.held_ref), custom_call_target="tpu_custom_call" | custom-call | tf_op jit(solution)/shard_map/pallas_call | solution.py:592
